TPU v7x, 256 devices: a whole 4x4x8 slice. The times are simulated.
256 devices in a mesh: blk: 8 (over y_lo, x), tile: 32 (over y_hi, z, core).
Axes of the slice: x: 4, y: 4 (y_hi: 2, y_lo: 2; y = y_hi * 2 + y_lo), z: 8, core: 2. Of those that a mesh axis runs over, the one named last changes fastest.
Arguments:
- qkv: bfloat16 [3, 8192, 4096], P(None, ('blk', 'tile')), may hold values from -33 to 33
- frame_clip: int32 [16], replicated, may hold values from 0 to 2, never falling along the last dimension, each value on 1 to 10 neighbouring positions
- w_out: bfloat16 [4096, 5120], P('tile'), may hold values from -0.5 to 0.5
Outputs:
- projected: bfloat16 [8192, 5120], P(('blk', 'tile'))
All inputs are finite; a program needn't handle non-finite values.
Results may differ from a plain program's by a relative error of at most 0.023.
Values may be sent and summed in bfloat16 or wider, within the bound.
A program may use at most 64 MiB of HBM per device.

v0:
```python
import math

import jax
import jax.numpy as jnp
from jax import lax
from jax.sharding import PartitionSpec as P

FRB = 2
TPF = 16


def clip_lookup(frames, frame_clip):
    table = jnp.arange(frame_clip.shape[0], dtype=jnp.int32)
    hits = (frames[..., None] == table).astype(jnp.int32)
    return jnp.sum(hits * frame_clip, axis=-1)


def on_device(qkv, frame_clip, w_out):
    tiles = lax.axis_size("tile")
    blk_index = lax.axis_index("blk")
    tok_dev = qkv.shape[1]
    head_dim = w_out.shape[0]
    tok_blk = tok_dev * tiles
    scale = 1.0 / math.sqrt(head_dim)
    local = lax.all_to_all(qkv, "tile", split_axis=2, concat_axis=1, tiled=True)
    queries = local[0]
    keys_all = local[1]
    values_all = local[2]
    rows = jnp.arange(tok_blk, dtype=jnp.int32)
    query_clip = clip_lookup(blk_index * FRB + rows % tok_dev // TPF, frame_clip)
    start_state = (
        jnp.full((tok_blk,), -1e30, jnp.float32),
        jnp.zeros((tok_blk,), jnp.float32),
        jnp.zeros((tok_blk, head_dim), jnp.float32),
    )
    carry = start_state
    key_piece = lax.all_gather(keys_all, "blk", axis=0, tiled=True)
    value_piece = lax.all_gather(values_all, "blk", axis=0, tiled=True)
    count = key_piece.shape[0]
    width = math.gcd(count, tok_blk)
    key_blocks = key_piece.reshape(count // width, width, head_dim)
    value_blocks = value_piece.reshape(count // width, width, head_dim)
    firsts = width * jnp.arange(count // width, dtype=jnp.int32)

    def advance(state, item):
        key_block, value_block, first = item
        index = first + jnp.arange(width, dtype=jnp.int32)
        key_clip = clip_lookup(index // tok_blk * FRB + index % tok_dev // TPF, frame_clip)
        allowed = query_clip[:, None] == key_clip[None, :]
        run_max, run_sum, run_acc = state
        scores = (
            jnp.einsum("qd,kd->qk", queries, key_block, preferred_element_type=jnp.float32) * scale
        )
        masked = jnp.where(allowed, scores, -1e30)
        new_max = jnp.maximum(run_max, jnp.max(masked, axis=1))
        weights = jnp.where(allowed, jnp.exp(scores - new_max[:, None]), 0.0)
        factor = jnp.exp(run_max - new_max)
        new_sum = run_sum * factor + jnp.sum(weights, axis=1)
        new_acc = run_acc * factor[:, None] + jnp.dot(
            weights.astype(jnp.bfloat16), value_block, preferred_element_type=jnp.float32
        )
        state = (new_max, new_sum, new_acc)
        return (state, None)

    carry, unused = lax.scan(advance, carry, (key_blocks, value_blocks, firsts))
    run_max, run_sum, run_acc = carry
    attn = (run_acc / run_sum[:, None]).astype(jnp.bfloat16)
    return lax.psum_scatter(
        jnp.dot(attn, w_out, preferred_element_type=jnp.float32).astype(jnp.bfloat16),
        "tile",
        scatter_dimension=0,
        tiled=True,
    )


def solution(mesh):
    in_specs = (P(None, ("blk", "tile"), None), P(), P("tile", None))
    out_specs = P(("blk", "tile"), None)
    return jax.shard_map(
        on_device, mesh=mesh, in_specs=in_specs, out_specs=out_specs, check_vma=False
    )
```

profile of v0, /device:TPU:1, one launch (start us, length us, event | category | flops | bytes accessed | tf_op | source)
XLA Modules:
  0.0 371.8 jit_solution(4900958124774167915)
XLA Ops:
  6.5 6.1 %copy.17 = bf16[3,32,4096]{1,0,2:T(4,128)(2,1)} copy(bf16[3,32,4096]{2,1,0:T(8,128)(2,1)} %param.5) | data formatting | bytes 1572864 | tf_op args[0]
  12.6 6.2 %reshape.88 = bf16[32,2,6144]{2,1,0:T(2,128)(2,1)S(1)} reshape(bf16[4096,3,32]{2,1,0:T(4,128)(2,1)} %bitcast.49) | data formatting | bytes 1572864
  18.8 35.3 %all_to_all.15 = bf16[32,2,6144]{2,1,0:T(2,128)(2,1)S(1)} all-to-all(bf16[32,2,6144]{2,1,0:T(2,128)(2,1)S(1)} %reshape.88), channel_id=1, replica_groups=mesh['blk'=8,'tile'=32] {'tile'}, dimensions={0} | all-to-all | bytes 1572864 | tf_op jit(solution)/shard_map/all_to_all | solution.py:25
  54.1 4.9 %reshape.89 = bf16[4096,3,32]{2,1,0:T(4,128)(2,1)} reshape(bf16[32,2,6144]{2,1,0:T(2,128)(2,1)S(1)} %all_to_all.15) | data formatting | bytes 1572864
  59.0 4.2 %copy.22 = bf16[3,32,32,128]{3,2,1,0:T(8,128)(2,1)S(1)} copy(bf16[3,32,32,128]{1,0,3,2:T(4,128)(2,1)} %bitcast.48) | data formatting | bytes 1572864 | tf_op jit(solution)/shard_map/all_to_all | solution.py:25
  65.3 34.5 %all-gather.5.cloned.1.call-done = bf16[8192,128]{1,0:T(8,128)(2,1)} async-done(((bf16[1024,128]{1,0:T(8,128)(2,1)}), bf16[8192,128]{1,0:T(8,128)(2,1)}) %all-gather.5.cloned.1.call-update) | async-done | bytes 2097168 | tf_op jit(solution)/shard_map/all_gather | solution.py:38
  99.8 45.2 %all-gather.3.cloned.1.call-done = bf16[8192,128]{1,0:T(8,128)(2,1)} async-done(((bf16[1024,128]{1,0:T(8,128)(2,1)}), bf16[8192,128]{1,0:T(8,128)(2,1)}) %all-gather.3.cloned.1.call-update) | async-done | bytes 2097168 | tf_op jit(solution)/shard_map/all_gather | solution.py:37
  145.0 50.5 %while.18 = (s32[]{:T(128)}, f32[1024]{0:T(1024)S(1)}, f32[1024]{0:T(1024)S(1)}, f32[1024,128]{1,0:T(8,128)S(1)}, s32[1024]{0:T(1024)S(1)}, /*index=5*/s32[8]{0:...) while((s32[]{:T(128)}, f32[1024]{0:T(1024)S(1)}, ...), condition=%wide.region_5.6_spmd.clone, body=%wide.region_1.5_spmd.clone.sunk | while | flops 552039424 | bytes 14520545 | solution.py:65
  146.3 1.7 fusion.53
  148.1 1.0 fusion.54
  149.1 2.2 fusion.56
  152.7 1.7 fusion.53
  154.4 1.0 fusion.54
  155.4 2.2 fusion.56
  159.0 1.7 fusion.53
  160.7 1.0 fusion.54
  161.7 2.2 fusion.56
  165.3 1.7 fusion.53
  167.0 1.0 fusion.54
  168.0 2.2 fusion.56
  171.6 1.7 fusion.53
  173.3 1.0 fusion.54
  174.3 2.2 fusion.56
  177.9 1.7 fusion.53
  179.6 1.0 fusion.54
  180.6 2.2 fusion.56
  184.2 1.7 fusion.53
  186.9 2.2 fusion.56
  190.5 1.7 fusion.53
  193.2 2.2 fusion.56
  195.5 5.6 %convolution_convert_fusion = bf16[1024,5120]{1,0:T(8,128)(2,1)} fusion(bf16[128,5120]{1,0:T(8,128)(2,1)S(1)} %copy-done, f32[1024,128]{1,0:T(8,128)S(1)} %get-tuple-element.169, f32[1024]{0:T(1024)S(1)} %get-tuple-element.170), kind=kOutput, calls=%fused_computation.49 | convolution fusion | flops 1347682304 | bytes 12324864 | tf_op jit(solution)/shard_map/dot_general | solution.py:69
  201.1 164.2 %reduce-scatter.2.cloned.1.call-done = bf16[32,5120]{1,0:T(8,128)(2,1)} async-done(((bf16[1024,5120]{1,0:T(8,128)(2,1)}), bf16[32,5120]{1,0:T(8,128)(2,1)}) %reduce-scatter.2.cloned.1.call-update) | async-done | bytes 327696 | tf_op jit(solution)/shard_map/reduce_scatter | solution.py:68
  (70 shorter events, 14.8 us)
Async XLA Ops:
  6.5 188.9 %copy-start = (bf16[128,5120]{1,0:T(8,128)(2,1)S(1)}, bf16[128,5120]{1,0:T(8,128)(2,1)}, u32[]{:S(2)}) copy-start(bf16[128,5120]{1,0:T(8,128)(2,1)} %param.7) | copy-start | bytes 3932164
  6.5 93.3 %all-gather.5.cloned.1.call-start = ((), (), s32[]{:S(2)}) async-start(), calls=%async_computation.3 | async-start | bytes 2359296 | tf_op jit(solution)/shard_map/all_gather | solution.py:38
  59.0 6.1 %copy-start.1 = (s32[16]{0:T(128)S(1)}, s32[16]{0:T(128)}, u32[]{:S(2)}) copy-start(s32[16]{0:T(128)} %param.6) | copy-start | bytes 196
  64.1 80.9 %all-gather.3.cloned.1.call-start = ((), (), s32[]{:S(2)}) async-start(), calls=%async_computation.2 | async-start | bytes 2359296 | tf_op jit(solution)/shard_map/all_gather | solution.py:37
  65.0 300.3 %reduce-scatter.2.cloned.1.call-start = ((), (), s32[]{:S(2)}) async-start(), calls=%async_computation.4 | async-start | bytes 10813440 | tf_op jit(solution)/shard_map/reduce_scatter | solution.py:68
Sparse Core Ops, SparseCore 0:
  64.3 35.5 all-gather.4
  101.6 43.3 all-gather.2
  201.2 164.0 reduce-scatter.1
where the time goes:
time: 376 us; the launch traced here: 372 us
  waiting for transfers between devices  244 us (65%)
  matrix products  37 us (10%)
  blocking collectives  35.3 us (9%)
  local copies, waits for them, and re-layouts  27.9 us (7%)
  other arithmetic  14 us (4%)
  between operations  13.2 us (4%)
    reduce_scatter x1, waiting for transfers between devices, on_device(): lax.psum_scatter(jnp.dot(attn, w_out, preferred_element_type=jnp.float32)...  164 us
    all_gather x1, waiting for transfers between devices, on_device(): key_piece = lax.all_gather(keys_all, 'blk', axis=0, tiled=True)  45.2 us
    all_to_all x1, blocking collectives, on_device(): local = lax.all_to_all(qkv, 'tile', split_axis=2, concat_axis=1, tiled=True)  35.3 us
    all_gather x1, waiting for transfers between devices, on_device(): value_piece = lax.all_gather(values_all, 'blk', axis=0, tiled=True)  34.5 us
    dot_general x8, matrix products, advance(): jnp.dot(weights.astype(jnp.bfloat16), value_block, preferred_element_type...  17.7 us
    unnamed x7, local copies, waits for them, and re-layouts  17.2 us
    dot_general x8, matrix products, advance(): jnp.einsum('qd,kd->qk', queries, key_block, preferred_element_type=jnp.fl...  13.6 us
    reduce_sum x8, other arithmetic, advance(): new_sum = run_sum * factor + jnp.sum(weights, axis=1)  7.79 us
  transfers between devices with their start and end apart: 3, of which 3 were waited for; matrix products, arithmetic and copies ran while one was open for 0% of the time, Pallas kernels for 0%

commit v1 on v0

v1 whole, which is shorter than its diff:
```python
import functools
import math

import jax
import jax.numpy as jnp
from jax import lax
from jax.experimental import pallas as pl
from jax.experimental.pallas import tpu as pltpu
from jax.sharding import PartitionSpec as P

MESH = pl.DeviceIdType.MESH
BF = jnp.bfloat16
F32 = jnp.float32
NEG = -1e30
NX, NY, NZ = 4, 4, 8
OFFS = (0, 1, 3, 2)


def place():
    b = lax.axis_index("blk")
    t = lax.axis_index("tile")
    return b % NX, b // NX, t // 16, (t // 2) % NZ, t % 2


def dev(x, y, z, c):
    return {"blk": (y % 2) * NX + x, "tile": (y // 2) * 16 + z * 2 + c}


def kernel(
    clip_ref, qkv_ref, w_in, out_ref,
    src, q_ref, kv, w_ref, m_ref, l_ref, acc_ref, o_ref, oa, ps, pr,
    lsem, a_send, a_recv, kv_send, kv_recv, w_send, w_recv,
    o_send, o_recv, oa_send, oa_recv, p_send, p_recv,
):
    x, ylo, yhi, z, c = place()
    y = yhi * 2 + ylo
    yp = NY - 1 - y
    sib = 1 - c
    cols = w_ref.shape[-1]
    coef = math.log2(math.e) / math.sqrt(128)

    def remote(s, d, ss, rs, device):
        return pltpu.make_async_remote_copy(
            src_ref=s, dst_ref=d, send_sem=ss, recv_sem=rs, device_id=device, device_id_type=MESH
        )

    def plane(n):
        return (y + n // NZ) % NY, (z + n % NZ) % NZ

    def column(yy, zz):
        return pl.multiple_of(((yy // 2) * 16 + zz * 2 + yy % 2) * 128, 128)

    load = pltpu.make_async_copy(qkv_ref, src, lsem.at[0])
    load.start()

    barrier = pltpu.get_barrier_semaphore()

    def greet(device):
        pl.semaphore_signal(barrier, inc=1, device_id=device, device_id_type=MESH)

    def greet_plane(n, carry):
        yy, zz = plane(n)
        greet(dev(x, yy, zz, c))
        return carry

    lax.fori_loop(1, NY * NZ, greet_plane, 0)
    greet(dev(x, y, z, sib))
    greet(dev(x, yp, z, sib))

    def greet_line(n, carry):
        xx = (x + n) % NX
        greet(dev(xx, y, z, c))
        greet(dev(xx, y, z, sib))
        greet(dev(xx, yp, z, c))
        greet(dev(xx, yp, z, sib))
        return carry

    lax.fori_loop(1, NX, greet_line, 0)
    load.wait()
    pl.semaphore_wait(barrier, NY * NZ - 1 + 2 + 4 * (NX - 1))

    row = pl.multiple_of((yhi * NZ + z) * 16, 16)

    def landing(k):
        if k == 0:
            return q_ref.at[ylo, :, pl.ds(row, 16), :]
        return kv.at[k - 1, ylo, pl.ds(2 * x, 2), c, pl.ds(row, 16), :]

    for k in (1, 2, 0):
        def send(n, carry, k=k):
            yy, zz = plane(n)
            remote(
                src.at[k, :, :, pl.ds(column(yy, zz), 128)], landing(k),
                a_send.at[k], a_recv.at[k], dev(x, yy, zz, c),
            ).start()
            return carry

        pltpu.make_async_copy(
            src.at[k, :, :, pl.ds(column(y, z), 128)], landing(k), a_recv.at[k]
        ).start()
        lax.fori_loop(1, NY * NZ, send, 0)

    def wcols(core):
        return pl.ds(pl.multiple_of((x * 2 + core) * cols, 128), cols)

    w_own = pltpu.make_async_copy(w_in.at[:, wcols(c)], w_ref.at[z, c], lsem.at[1])
    w_own.start()
    w_sib = remote(
        w_in.at[:, wcols(sib)], w_ref.at[z, c], w_send.at[0], w_recv.at[0], dev(x, y, z, sib)
    )
    w_sib.start()

    def region(k, r, core):
        return kv.at[k, :, pl.ds(2 * ((x - r + NX) % NX), 2), core]

    kv_copies = []

    def share(k, r):
        copy = remote(
            region(k, r, c), region(k, r, c), kv_send.at[k, 3 + r], kv_recv.at[k, 3 + r],
            dev(x, y, z, sib),
        )
        copy.start()
        kv_copies.append(copy)

    for k in range(2):
        pltpu.make_async_copy(region(k, 0, c), region(k, 0, c), a_recv.at[k + 1]).wait()
        for r in (1, 3, 2):
            copy = remote(
                region(k, 0, c), region(k, 0, c), kv_send.at[k, r - 1], kv_recv.at[k, r - 1],
                dev((x + r) % NX, y, z, c),
            )
            copy.start()
            kv_copies.append(copy)
        share(k, 0)
    pltpu.make_async_copy(q_ref, q_ref, a_recv.at[0]).wait()

    w_own.wait()
    w_sib.wait_recv()
    w_copies = []

    def hop_up(s):
        block = w_ref.at[(z - s + NZ) % NZ]
        copy = remote(block, block, w_send.at[1 + s], w_recv.at[1 + s], dev(x, y, (z + 1) % NZ, c))
        copy.start()
        w_copies.append(copy)

    def hop_down(s):
        block = w_ref.at[(z + s) % NZ]
        copy = remote(block, block, w_send.at[5 + s], w_recv.at[5 + s], dev(x, y, (z + NZ - 1) % NZ, c))
        copy.start()
        w_copies.append(copy)

    def w_wait(slot, block):
        pltpu.make_async_copy(w_ref.at[block], w_ref.at[block], w_recv.at[slot]).wait()

    def forward(s):
        w_wait(s, (z - s + NZ) % NZ)
        if s < 4:
            hop_up(s)
        if s < 4:
            w_wait(4 + s, (z + s) % NZ)
            if s < 3:
                hop_down(s)

    hop_up(0)
    hop_down(0)

    m_ref[...] = jnp.full_like(m_ref, NEG)
    l_ref[...] = jnp.zeros_like(l_ref)
    acc_ref[...] = jnp.zeros_like(acc_ref)

    for step, r in enumerate(OFFS):
        if r:
            for k in range(2):
                pltpu.make_async_copy(
                    region(k, r, c), region(k, r, c), kv_recv.at[k, r - 1]
                ).wait()
                share(k, r)
        for k in range(2):
            pltpu.make_async_copy(
                region(k, r, sib), region(k, r, sib), kv_recv.at[k, 3 + r]
            ).wait()
        if step:
            forward(step)
        xs = (x - r + NX) % NX

        def frame(n, carry, xs=xs):
            half = n // 2
            g = 2 * xs + n % 2
            key_clip = clip_ref[half * 8 + g]
            keys = kv[0, half, g].reshape(512, 128)
            values = kv[1, half, g].reshape(512, 128)
            for j in range(4):
                kept = key_clip == clip_ref[(j // 2) * 8 + 2 * x + j % 2]
                s = lax.dot_general(
                    q_ref[j // 2, j % 2], keys, (((1,), (1,)), ((), ())),
                    preferred_element_type=F32,
                ) * coef
                top = jnp.max(s, axis=1, keepdims=True)
                old = m_ref[j]
                new = jnp.where(kept, jnp.maximum(old, top), old)
                shift = jnp.where(kept, new, -NEG)
                p = jnp.exp2(s - shift[:, :1])
                alpha = jnp.exp2(old - new)
                m_ref[j] = new
                l_ref[j] = l_ref[j] * alpha + jnp.sum(p, axis=1, keepdims=True)
                acc_ref[j] = acc_ref[j] * alpha + jnp.dot(
                    p.astype(BF), values, preferred_element_type=F32
                )
            return carry

        lax.fori_loop(0, 4, frame, 0)
    forward(4)

    for j in range(4):
        o = (acc_ref[j] / l_ref[j]).astype(BF)
        for yh in range(2):
            o_ref[(j // 2) ^ yh, :, yh, j % 2] = o[yh * 128:(yh + 1) * 128].reshape(NZ, 16, 128)

    me = x * 2 + c
    head = pl.multiple_of((z * 2 + ylo) * 128, 128)
    o_land = oa.at[me, :, :, :, pl.ds(head, 128)]

    def o_target(n):
        pair = ((ylo ^ yhi) + n // NZ) % 2
        return pair, (z + n % NZ) % NZ

    def o_move(n, carry):
        pair, zz = o_target(n)
        remote(
            o_ref.at[pair, zz], o_land, o_send, o_recv, dev(x, yhi * 2 + (pair ^ yhi), zz, c)
        ).start()
        return carry

    pltpu.make_async_copy(o_ref.at[ylo ^ yhi, z], o_land, o_recv).start()
    lax.fori_loop(1, 2 * NZ, o_move, 0)
    pltpu.make_async_copy(oa.at[me], oa.at[me], o_recv).wait()

    oa_copies = []

    def oa_slot(r, core):
        return oa.at[((x - r + NX) % NX) * 2 + core]

    def oa_copy(r, slot, device):
        copy = remote(oa_slot(r, c), oa_slot(r, c), oa_send.at[slot], oa_recv.at[slot], device)
        copy.start()
        oa_copies.append(copy)

    for r in (1, 3, 2):
        oa_copy(0, r - 1, dev((x + r) % NX, y, z, c))
    oa_copy(0, 3, dev(x, y, z, sib))

    for r in OFFS:
        if r:
            pltpu.make_async_copy(oa_slot(r, c), oa_slot(r, c), oa_recv.at[r - 1]).wait()
            oa_copy(r, 3 + r, dev(x, y, z, sib))
        pltpu.make_async_copy(oa_slot(r, sib), oa_slot(r, sib), oa_recv.at[3 + r]).wait()
        xs = (x - r + NX) % NX
        rows = oa[pl.ds(2 * xs, 2)].reshape(128, 2048)
        part = jnp.dot(rows, w_ref[...].reshape(2048, cols), preferred_element_type=F32)
        ps[pl.ds(4 * xs, 4)] = part.astype(BF).reshape(4, 32, cols)
        for core in range(2):
            for yh in range(2):
                spot = ps.at[4 * xs + 2 * core + yh]
                land = pr.at[yhi, :, wcols(c)]
                if r == 0:
                    here = jnp.logical_and(core == c, yh == yhi)

                    @pl.when(here)
                    def _():
                        pltpu.make_async_copy(spot, land, p_recv).start()

                    @pl.when(jnp.logical_not(here))
                    def _():
                        remote(
                            spot, land, p_send, p_recv,
                            dev(xs, yh * 2 + ((ylo ^ yhi) ^ yh), z, core),
                        ).start()
                else:
                    remote(
                        spot, land, p_send, p_recv,
                        dev(xs, yh * 2 + ((ylo ^ yhi) ^ yh), z, core),
                    ).start()
    pltpu.make_async_copy(pr, pr, p_recv).wait()
    out_ref[...] = (pr[0].astype(F32) + pr[1].astype(F32)).astype(BF)

    for k in range(3):
        sent = src.at[k, :, :, pl.ds(0, (NY * NZ - 1) * 128)]
        pltpu.make_async_copy(sent, sent, a_send.at[k]).wait()
    w_sib.wait_send()
    for copy in kv_copies + w_copies + oa_copies:
        copy.wait_send()
    sent = oa.at[0, :, :, :, pl.ds(0, (2 * NZ - 1) * 128)]
    pltpu.make_async_copy(sent, sent, o_send).wait()
    sent = ps.at[pl.ds(0, 15)]
    pltpu.make_async_copy(sent, sent, p_send).wait()


def on_device(qkv, frame_clip, w_out):
    parts, tokens, width = qkv.shape
    rows, columns = w_out.shape
    cols = columns // 8
    dma = pltpu.SemaphoreType.DMA
    return pl.pallas_call(
        kernel,
        out_shape=jax.ShapeDtypeStruct((tokens, columns), BF),
        in_specs=[
            pl.BlockSpec(memory_space=pltpu.SMEM),
            pl.BlockSpec(memory_space=pl.ANY),
            pl.BlockSpec(memory_space=pl.ANY),
        ],
        out_specs=pl.BlockSpec(memory_space=pltpu.VMEM),
        scratch_shapes=[
            pltpu.VMEM((3, 2, 16, width), BF),
            pltpu.VMEM((2, 2, 256, 128), BF),
            pltpu.VMEM((2, 2, 8, 2, 256, 128), BF),
            pltpu.VMEM((NZ, 2, rows, cols), BF),
            pltpu.VMEM((4, 256, 128), F32),
            pltpu.VMEM((4, 256, 128), F32),
            pltpu.VMEM((4, 256, 128), F32),
            pltpu.VMEM((2, NZ, 2, 2, 16, 128), BF),
            pltpu.VMEM((8, 2, 2, 16, 2048), BF),
            pltpu.VMEM((16, 32, cols), BF),
            pltpu.VMEM((2, tokens, columns), BF),
            dma((2,)), dma((3,)), dma((3,)), dma((2, 7)), dma((2, 7)), dma((8,)), dma((8,)),
            dma, dma, dma((7,)), dma((7,)), dma, dma,
        ],
        compiler_params=pltpu.CompilerParams(
            collective_id=0, has_side_effects=True, vmem_limit_bytes=48 << 20
        ),
        name="attend_and_project",
    )(frame_clip, qkv.reshape(parts, 2, tokens // 2, width), w_out)


def solution(mesh):
    in_specs = (P(None, ("blk", "tile"), None), P(), P("tile", None))
    out_specs = P(("blk", "tile"), None)
    return jax.shard_map(
        on_device, mesh=mesh, in_specs=in_specs, out_specs=out_specs, check_vma=False
    )
```

time: 376 us -> 109 us (0.29); the launches traced: 372 us -> 109 us
  waiting for transfers between devices: 244 us -> 0 us
  Pallas kernels: 0 us -> 105 us
  matrix products: 37 us -> 0 us
  blocking collectives: 35.3 us -> 0 us
  local copies, waits for them, and re-layouts: 27.9 us -> 3.83 us
  other arithmetic: 14 us -> 0 us
  between operations: 13.2 us -> 0.01 us
    reduce_scatter x1 -> x0, waiting for transfers between devices: 164 us -> none  [on_device(): lax.psum_scatter(jnp.dot(attn, w_out, preferred_element_type=jnp.float32)...]
    pallas_call x0 -> x1, Pallas kernels: none -> 105 us  [on_device(): pl.pallas_call(kernel, out_shape=jax.ShapeDtypeStruct((tokens, columns),...]
    all_gather x2 -> x0, waiting for transfers between devices: 79.7 us -> none  [the longest x1 45.2 us: on_device(): key_piece = lax.all_gather(keys_all, 'blk', axis=0, tiled=True)]
    dot_general x17 -> x0, matrix products: 37 us -> none  [the longest x8 17.7 us: advance(): jnp.dot(weights.astype(jnp.bfloat16), value_block, preferred_element_type...]
    all_to_all x1 -> x0, blocking collectives: 35.3 us -> none  [on_device(): local = lax.all_to_all(qkv, 'tile', split_axis=2, concat_axis=1, tiled=True)]
    unnamed x7, local copies, waits for them, and re-layouts: 17.2 us -> 3.83 us
    reduce_sum x17 -> x0, other arithmetic: 8.54 us -> none  [the longest x8 7.79 us: advance(): new_sum = run_sum * factor + jnp.sum(weights, axis=1)]
    add x17 -> x0, other arithmetic: 5.4 us -> none  [the longest x8 5.29 us: advance(): index // tok_blk * FRB + index % tok_dev // TPF]
  transfers between devices with their start and end apart: 3 -> 0, of which waited for: 3 -> 0; matrix products, arithmetic and copies ran while one was open for 0% -> 0% of each run, Pallas kernels for 0% -> 0%
where the time goes in v1:
time: 109 us
  Pallas kernels  105 us (96%)
  local copies, waits for them, and re-layouts  3.83 us (4%)
    pallas_call x1, Pallas kernels, on_device(): pl.pallas_call(kernel, out_shape=jax.ShapeDtypeStruct((tokens, columns),...  105 us
    unnamed x7, local copies, waits for them, and re-layouts  3.83 us

profile of v1, /device:TPU:1, one launch (start us, length us, event | category | flops | bytes accessed | tf_op | source)
XLA Modules:
  0.0 109.1 jit_solution(9940751239314352267)
XLA Ops:
  0.0 0.0 copy-start
  0.0 1.3 %copy-done = bf16[128,5120]{1,0:T(8,128)(2,1)S(1)} copy-done((bf16[128,5120]{1,0:T(8,128)(2,1)S(1)}, bf16[128,5120]{1,0:T(8,128)(2,1)}, u32[]{:S(2)}) %copy-start) | copy-done | bytes 1310744
  1.3 0.0 copy-start.1
  1.3 1.1 %copy-done.1 = bf16[3,32,4096]{2,1,0:T(8,128)(2,1)S(1)} copy-done((bf16[3,32,4096]{2,1,0:T(8,128)(2,1)S(1)}, bf16[3,32,4096]{2,1,0:T(8,128)(2,1)}, u32[]{:S(2)}) %copy-start.1) | copy-done | bytes 786456
  2.5 0.0 copy-start.2
  2.5 0.7 copy-done.2
  3.1 105.2 %attend_and_project.1 = bf16[32,5120]{1,0:T(8,128)(2,1)S(1)} custom-call(s32[16]{0:T(128)S(1)} %copy-done.2, bf16[3,2,16,4096]{3,2,1,0:T(8,128)(2,1)S(1)} %bitcast.1, bf16[128,5120]{1,0:T(8,128)(2,1)S(1)} %copy-done), custom_call_target="tpu_custom_call" | custom-call | tf_op jit(solution)/shard_map/attend_and_project/pallas_call | solution.py:305
  108.4 0.7 copy.5
Async XLA Ops:
  0.0 1.3 %copy-start = (bf16[128,5120]{1,0:T(8,128)(2,1)S(1)}, bf16[128,5120]{1,0:T(8,128)(2,1)}, u32[]{:S(2)}) copy-start(bf16[128,5120]{1,0:T(8,128)(2,1)} %w_in.1) | copy-start | bytes 3932164
  1.3 1.1 %copy-start.1 = (bf16[3,32,4096]{2,1,0:T(8,128)(2,1)S(1)}, bf16[3,32,4096]{2,1,0:T(8,128)(2,1)}, u32[]{:S(2)}) copy-start(bf16[3,32,4096]{2,1,0:T(8,128)(2,1)} %param.3) | copy-start | bytes 2359300
  2.5 0.7 copy-start.2

commit v2 on v1

--- a/solution.py
+++ b/solution.py
@@ -28,7 +28,7 @@
 
 def kernel(
     clip_ref, qkv_ref, w_in, out_ref,
-    src, q_ref, kv, w_ref, m_ref, l_ref, acc_ref, o_ref, oa, ps, pr,
+    src, q_ref, kv, w_ref, m_ref, acc_ref, o_ref, oa, ps, pr,
     lsem, a_send, a_recv, kv_send, kv_recv, w_send, w_recv,
     o_send, o_recv, oa_send, oa_recv, p_send, p_recv,
 ):
@@ -44,8 +44,11 @@
             src_ref=s, dst_ref=d, send_sem=ss, recv_sem=rs, device_id=device, device_id_type=MESH
         )
 
+    def hop(k):
+        return jnp.where(k % 2 == 0, k // 2, NZ - (k + 1) // 2)
+
     def plane(n):
-        return (y + n // NZ) % NY, (z + n % NZ) % NZ
+        return (y + n % NY) % NY, (z + hop(n // NY)) % NZ
 
     def column(yy, zz):
         return pl.multiple_of(((yy // 2) * 16 + zz * 2 + yy % 2) * 128, 128)
@@ -86,8 +89,8 @@
             return q_ref.at[ylo, :, pl.ds(row, 16), :]
         return kv.at[k - 1, ylo, pl.ds(2 * x, 2), c, pl.ds(row, 16), :]
 
-    for k in (1, 2, 0):
-        def send(n, carry, k=k):
+    def scatter(k):
+        def send(n, carry):
             yy, zz = plane(n)
             remote(
                 src.at[k, :, :, pl.ds(column(yy, zz), 128)], landing(k),
@@ -100,6 +103,9 @@
         ).start()
         lax.fori_loop(1, NY * NZ, send, 0)
 
+    scatter(1)
+    scatter(2)
+
     def wcols(core):
         return pl.ds(pl.multiple_of((x * 2 + core) * cols, 128), cols)
 
@@ -115,106 +121,132 @@
 
     kv_copies = []
 
-    def share(k, r):
+    def spread(k, r, slot, device):
         copy = remote(
-            region(k, r, c), region(k, r, c), kv_send.at[k, 3 + r], kv_recv.at[k, 3 + r],
-            dev(x, y, z, sib),
+            region(k, r, c), region(k, r, c), kv_send.at[k, slot], kv_recv.at[k, slot], device
         )
         copy.start()
         kv_copies.append(copy)
 
-    for k in range(2):
+    def share(k, r):
+        spread(k, r, 3 + r, dev(x, y, z, sib))
+
+    def arrived(k, r, core, slot):
+        pltpu.make_async_copy(
+            region(k, r, core), region(k, r, core), kv_recv.at[k, slot]
+        ).wait()
+
+    right, left = dev((x + 1) % NX, y, z, c), dev((x + NX - 1) % NX, y, z, c)
+
+    def neighbours(k):
         pltpu.make_async_copy(region(k, 0, c), region(k, 0, c), a_recv.at[k + 1]).wait()
-        for r in (1, 3, 2):
-            copy = remote(
-                region(k, 0, c), region(k, 0, c), kv_send.at[k, r - 1], kv_recv.at[k, r - 1],
-                dev((x + r) % NX, y, z, c),
-            )
-            copy.start()
-            kv_copies.append(copy)
+        spread(k, 0, 0, right)
+        spread(k, 0, 2, left)
         share(k, 0)
-    pltpu.make_async_copy(q_ref, q_ref, a_recv.at[0]).wait()
 
     w_own.wait()
     w_sib.wait_recv()
     w_copies = []
-
-    def hop_up(s):
-        block = w_ref.at[(z - s + NZ) % NZ]
-        copy = remote(block, block, w_send.at[1 + s], w_recv.at[1 + s], dev(x, y, (z + 1) % NZ, c))
+    twin = dev(x, yhi * 2 + 1 - ylo, z, c)
+
+    def w_copy(block, half, slot, device):
+        spot = w_ref.at[block, half]
+        copy = remote(spot, spot, w_send.at[slot], w_recv.at[slot], device)
         copy.start()
         w_copies.append(copy)
 
-    def hop_down(s):
-        block = w_ref.at[(z + s) % NZ]
-        copy = remote(block, block, w_send.at[5 + s], w_recv.at[5 + s], dev(x, y, (z + NZ - 1) % NZ, c))
-        copy.start()
-        w_copies.append(copy)
-
-    def w_wait(slot, block):
-        pltpu.make_async_copy(w_ref.at[block], w_ref.at[block], w_recv.at[slot]).wait()
+    def w_wait(block, half, slot):
+        spot = w_ref.at[block, half]
+        pltpu.make_async_copy(spot, spot, w_recv.at[slot]).wait()
+
+    def above(s):
+        return (z + s) % NZ
+
+    def below(s):
+        return (z - s + NZ) % NZ
 
     def forward(s):
-        w_wait(s, (z - s + NZ) % NZ)
+        if s:
+            w_wait(below(s), ylo, s)
+            w_copy(below(s), ylo, 7 + s, twin)
+            if s < 4:
+                w_wait(above(s), ylo, 4 + s)
+                w_copy(above(s), ylo, 11 + s, twin)
         if s < 4:
-            hop_up(s)
-        if s < 4:
-            w_wait(4 + s, (z + s) % NZ)
-            if s < 3:
-                hop_down(s)
-
-    hop_up(0)
-    hop_down(0)
+            w_copy(below(s), ylo, 1 + s, dev(x, y, above(1), c))
+        if s < 3:
+            w_copy(above(s), ylo, 5 + s, dev(x, y, below(1), c))
+
+    def w_finish():
+        for s in range(1, 5):
+            w_wait(below(s), 1 - ylo, 7 + s)
+            if s < 4:
+                w_wait(above(s), 1 - ylo, 11 + s)
+
+    neighbours(0)
+    scatter(0)
+    forward(0)
+    neighbours(1)
+    arrived(0, 1, c, 0)
+    spread(0, 1, 1, right)
+    share(0, 1)
+    arrived(0, 3, c, 2)
+    share(0, 3)
+    arrived(1, 3, c, 2)
+    spread(1, 3, 1, left)
+    share(1, 3)
+    arrived(1, 1, c, 0)
+    share(1, 1)
+    pltpu.make_async_copy(q_ref, q_ref, a_recv.at[0]).wait()
 
     m_ref[...] = jnp.full_like(m_ref, NEG)
-    l_ref[...] = jnp.zeros_like(l_ref)
     acc_ref[...] = jnp.zeros_like(acc_ref)
 
     for step, r in enumerate(OFFS):
-        if r:
-            for k in range(2):
-                pltpu.make_async_copy(
-                    region(k, r, c), region(k, r, c), kv_recv.at[k, r - 1]
-                ).wait()
-                share(k, r)
         for k in range(2):
-            pltpu.make_async_copy(
-                region(k, r, sib), region(k, r, sib), kv_recv.at[k, 3 + r]
-            ).wait()
+            arrived(k, r, sib, 3 + r)
         if step:
             forward(step)
+        if step == 2:
+            for k in range(2):
+                arrived(k, 2, c, 1)
+                share(k, 2)
         xs = (x - r + NX) % NX
 
-        def frame(n, carry, xs=xs):
-            half = n // 2
-            g = 2 * xs + n % 2
-            key_clip = clip_ref[half * 8 + g]
-            keys = kv[0, half, g].reshape(512, 128)
-            values = kv[1, half, g].reshape(512, 128)
+        def block(half, carry, xs=xs):
+            keys = kv[0, half, pl.ds(2 * xs, 2)].reshape(1024, 128)
+            values = kv[1, half, pl.ds(2 * xs, 2)].reshape(1024, 128)
+            values = jnp.concatenate([values, jnp.ones_like(values)], axis=1)
             for j in range(4):
-                kept = key_clip == clip_ref[(j // 2) * 8 + 2 * x + j % 2]
+                query_clip = clip_ref[(j // 2) * 8 + 2 * x + j % 2]
+                kept = [query_clip == clip_ref[half * 8 + 2 * xs + i] for i in range(2)]
                 s = lax.dot_general(
                     q_ref[j // 2, j % 2], keys, (((1,), (1,)), ((), ())),
                     preferred_element_type=F32,
-                ) * coef
-                top = jnp.max(s, axis=1, keepdims=True)
+                )
+                s = [s[:, :512], s[:, 512:]]
+                tops = [
+                    jnp.where(kept[i], jnp.max(s[i], axis=1, keepdims=True), NEG)
+                    for i in range(2)
+                ]
                 old = m_ref[j]
-                new = jnp.where(kept, jnp.maximum(old, top), old)
-                shift = jnp.where(kept, new, -NEG)
-                p = jnp.exp2(s - shift[:, :1])
+                new = jnp.maximum(old, jnp.maximum(tops[0], tops[1]) * coef)
                 alpha = jnp.exp2(old - new)
                 m_ref[j] = new
-                l_ref[j] = l_ref[j] * alpha + jnp.sum(p, axis=1, keepdims=True)
-                acc_ref[j] = acc_ref[j] * alpha + jnp.dot(
-                    p.astype(BF), values, preferred_element_type=F32
+                p = [
+                    jnp.exp2(s[i] * coef - jnp.where(kept[i], new, -NEG)[:, :1]).astype(BF)
+                    for i in range(2)
+                ]
+                acc_ref[j] = acc_ref[j] * jnp.concatenate([alpha, alpha], axis=1) + jnp.dot(
+                    jnp.concatenate(p, axis=1), values, preferred_element_type=F32
                 )
             return carry
 
-        lax.fori_loop(0, 4, frame, 0)
-    forward(4)
+        lax.fori_loop(0, 2, block, 0)
 
     for j in range(4):
-        o = (acc_ref[j] / l_ref[j]).astype(BF)
+        acc = acc_ref[j]
+        o = (acc[:, :128] / acc[:, 128:]).astype(BF)
         for yh in range(2):
             o_ref[(j // 2) ^ yh, :, yh, j % 2] = o[yh * 128:(yh + 1) * 128].reshape(NZ, 16, 128)
 
@@ -223,8 +255,8 @@
     o_land = oa.at[me, :, :, :, pl.ds(head, 128)]
 
     def o_target(n):
-        pair = ((ylo ^ yhi) + n // NZ) % 2
-        return pair, (z + n % NZ) % NZ
+        pair = ((ylo ^ yhi) + n % 2) % 2
+        return pair, (z + hop(n // 2)) % NZ
 
     def o_move(n, carry):
         pair, zz = o_target(n)
@@ -239,23 +271,48 @@
 
     oa_copies = []
 
-    def oa_slot(r, core):
-        return oa.at[((x - r + NX) % NX) * 2 + core]
-
-    def oa_copy(r, slot, device):
-        copy = remote(oa_slot(r, c), oa_slot(r, c), oa_send.at[slot], oa_recv.at[slot], device)
+    def oa_slot(r, core, h=None):
+        slot = oa.at[((x - r + NX) % NX) * 2 + core]
+        return slot if h is None else slot.at[h]
+
+    def oa_copy(r, h, slot, device):
+        copy = remote(
+            oa_slot(r, c, h), oa_slot(r, c, h), oa_send.at[slot], oa_recv.at[slot], device
+        )
         copy.start()
         oa_copies.append(copy)
 
-    for r in (1, 3, 2):
-        oa_copy(0, r - 1, dev((x + r) % NX, y, z, c))
-    oa_copy(0, 3, dev(x, y, z, sib))
+    def oa_arrived(r, core, h, slot):
+        pltpu.make_async_copy(
+            oa_slot(r, core, h), oa_slot(r, core, h), oa_recv.at[slot]
+        ).wait()
+
+    for h in range(2):
+        oa_copy(0, h, 3 * h, right)
+        oa_copy(0, h, 3 * h + 2, left)
+    oa_copy(0, None, 6, dev(x, y, z, sib))
+
+    forward(4)
 
     for r in OFFS:
+        if r == 0:
+            oa_arrived(0, sib, None, 6)
+            w_finish()
+        if r == 1:
+            oa_arrived(1, c, 0, 0)
+            oa_copy(1, 0, 1, right)
+            oa_arrived(3, c, 1, 5)
+            oa_copy(3, 1, 4, left)
+            oa_arrived(1, c, 1, 3)
+            oa_copy(1, None, 7, dev(x, y, z, sib))
+            oa_arrived(3, c, 0, 2)
+            oa_copy(3, None, 9, dev(x, y, z, sib))
+        if r == 2:
+            oa_arrived(2, c, 0, 1)
+            oa_arrived(2, c, 1, 4)
+            oa_copy(2, None, 8, dev(x, y, z, sib))
         if r:
-            pltpu.make_async_copy(oa_slot(r, c), oa_slot(r, c), oa_recv.at[r - 1]).wait()
-            oa_copy(r, 3 + r, dev(x, y, z, sib))
-        pltpu.make_async_copy(oa_slot(r, sib), oa_slot(r, sib), oa_recv.at[3 + r]).wait()
+            oa_arrived(r, sib, None, 6 + r)
         xs = (x - r + NX) % NX
         rows = oa[pl.ds(2 * xs, 2)].reshape(128, 2048)
         part = jnp.dot(rows, w_ref[...].reshape(2048, cols), preferred_element_type=F32)
@@ -317,17 +374,16 @@
             pltpu.VMEM((2, 2, 8, 2, 256, 128), BF),
             pltpu.VMEM((NZ, 2, rows, cols), BF),
             pltpu.VMEM((4, 256, 128), F32),
-            pltpu.VMEM((4, 256, 128), F32),
-            pltpu.VMEM((4, 256, 128), F32),
+            pltpu.VMEM((4, 256, 256), F32),
             pltpu.VMEM((2, NZ, 2, 2, 16, 128), BF),
             pltpu.VMEM((8, 2, 2, 16, 2048), BF),
             pltpu.VMEM((16, 32, cols), BF),
             pltpu.VMEM((2, tokens, columns), BF),
-            dma((2,)), dma((3,)), dma((3,)), dma((2, 7)), dma((2, 7)), dma((8,)), dma((8,)),
-            dma, dma, dma((7,)), dma((7,)), dma, dma,
+            dma((2,)), dma((3,)), dma((3,)), dma((2, 7)), dma((2, 7)), dma((15,)), dma((15,)),
+            dma, dma, dma((10,)), dma((10,)), dma, dma,
         ],
         compiler_params=pltpu.CompilerParams(
-            collective_id=0, has_side_effects=True, vmem_limit_bytes=48 << 20
+            collective_id=0, has_side_effects=True, vmem_limit_bytes=66_400_000
         ),
         name="attend_and_project",
     )(frame_clip, qkv.reshape(parts, 2, tokens // 2, width), w_out)

time: 109 us -> 88.4 us (0.81)
  Pallas kernels: 105 us -> 86.5 us
  local copies, waits for them, and re-layouts: 3.83 us -> 1.72 us
    pallas_call x1, Pallas kernels: 105 us -> 86.5 us  [on_device(): pl.pallas_call(kernel, out_shape=jax.ShapeDtypeStruct((tokens, columns),...]
    unnamed x7 -> x1, local copies, waits for them, and re-layouts: 3.83 us -> 1.72 us
where the time goes in v2:
time: 88.4 us; the launch traced here: 88.2 us
  Pallas kernels  86.5 us (98%)
  local copies, waits for them, and re-layouts  1.72 us (2%)
    pallas_call x1, Pallas kernels, on_device(): pl.pallas_call(kernel, out_shape=jax.ShapeDtypeStruct((tokens, columns),...  86.5 us

profile of v2, /device:TPU:1, one launch (start us, length us, event | category | flops | bytes accessed | tf_op | source)
XLA Modules:
  0.0 88.2 jit_solution(4647746634888446722)
XLA Ops:
  0.0 86.5 %attend_and_project.1 = bf16[32,5120]{1,0:T(8,128)(2,1)} custom-call(s32[16]{0:T(128)} %clip_ref.1, bf16[3,2,16,4096]{3,2,1,0:T(8,128)(2,1)} %bitcast.1, bf16[128,5120]{1,0:T(8,128)(2,1)} %w_in.1), custom_call_target="tpu_custom_call" | custom-call | tf_op jit(solution)/shard_map/attend_and_project/pallas_call | solution.py:362
  86.5 1.7 %copy.5 = bf16[32,5120]{1,0:T(8,128)(2,1)} copy(bf16[32,5120]{1,0:T(8,128)(2,1)} %attend_and_project.1) | data formatting | bytes 655360

commit v3 on v2

v3 whole, which is shorter than its diff:
```python
import functools
import math

import jax
import jax.numpy as jnp
from jax import lax
from jax.experimental import pallas as pl
from jax.experimental.pallas import tpu as pltpu
from jax.sharding import PartitionSpec as P

MESH = pl.DeviceIdType.MESH
BF = jnp.bfloat16
F32 = jnp.float32
NEG = -1e30
NX, NY, NZ = 4, 4, 8


def place():
    b = lax.axis_index("blk")
    t = lax.axis_index("tile")
    return b % NX, b // NX, t // 16, (t // 2) % NZ, t % 2


def dev(x, y, z, c):
    return {"blk": (y % 2) * NX + x, "tile": (y // 2) * 16 + z * 2 + c}


def kernel(
    clip_ref, qkv_ref, w_in, pr,
    src, q_ref, kv, w_ref, m_ref, acc_ref, o_ref, oa, ps,
    lsem, a_send, a_recv, kv_send, kv_recv, w_send, w_recv,
    o_send, o_recv, oa_send, oa_recv, p_send, p_recv,
):
    x, ylo, yhi, z, c = place()
    y = yhi * 2 + ylo
    yp = NY - 1 - y
    sib = 1 - c
    cols = w_ref.shape[-1]
    coef = math.log2(math.e) / math.sqrt(128)

    def remote(s, d, ss, rs, device):
        return pltpu.make_async_remote_copy(
            src_ref=s, dst_ref=d, send_sem=ss, recv_sem=rs, device_id=device, device_id_type=MESH
        )

    def hop(k):
        return jnp.where(k % 2 == 0, k // 2, NZ - (k + 1) // 2)

    def plane(n):
        return (y + n % NY) % NY, (z + hop(n // NY)) % NZ

    def column(yy, zz):
        return pl.multiple_of(((yy // 2) * 16 + zz * 2 + yy % 2) * 128, 128)

    load = pltpu.make_async_copy(qkv_ref, src, lsem.at[0])
    load.start()

    barrier = pltpu.get_barrier_semaphore()

    def greet(device):
        pl.semaphore_signal(barrier, inc=1, device_id=device, device_id_type=MESH)

    def greet_plane(n, carry):
        yy, zz = plane(n)
        greet(dev(x, yy, zz, c))
        return carry

    lax.fori_loop(1, NY * NZ, greet_plane, 0)
    greet(dev(x, y, z, sib))
    greet(dev(x, yp, z, sib))

    def greet_line(n, carry):
        xx = (x + n) % NX
        greet(dev(xx, y, z, c))
        greet(dev(xx, y, z, sib))
        greet(dev(xx, yp, z, c))
        greet(dev(xx, yp, z, sib))
        return carry

    lax.fori_loop(1, NX, greet_line, 0)
    load.wait()
    pl.semaphore_wait(barrier, NY * NZ - 1 + 2 + 4 * (NX - 1))

    row = pl.multiple_of((yhi * NZ + z) * 16, 16)

    def cut(k, column):
        if k == 2:
            return src.at[0, :, :, pl.ds(column, 128)]
        return src.at[1:3, k, :, pl.ds(column, 128)]

    def landing(k):
        if k == 2:
            return q_ref.at[ylo, :, pl.ds(row, 16), :]
        return kv.at[:, ylo, 2 * x + k, c, pl.ds(row, 16), :]

    def scatter(k):
        def send(n, carry):
            yy, zz = plane(n)
            remote(
                cut(k, column(yy, zz)), landing(k), a_send.at[k], a_recv.at[k],
                dev(x, yy, zz, c),
            ).start()
            return carry

        pltpu.make_async_copy(cut(k, column(y, z)), landing(k), a_recv.at[k]).start()
        lax.fori_loop(1, NY * NZ, send, 0)

    scatter(0)
    scatter(2)
    scatter(1)

    def wcols(core):
        return pl.ds(pl.multiple_of((x * 2 + core) * cols, 128), cols)

    w_own = pltpu.make_async_copy(w_in.at[:, wcols(c)], w_ref.at[z, c], lsem.at[1])
    w_own.start()
    w_sib = remote(
        w_in.at[:, wcols(sib)], w_ref.at[z, c], w_send.at[0], w_recv.at[0], dev(x, y, z, sib)
    )
    w_sib.start()

    def piece(k, i, r, core):
        return kv.at[k, :, 2 * ((x - r + NX) % NX) + i, core]

    def spread(k, i, r, slot, device):
        remote(
            piece(k, i, r, c), piece(k, i, r, c), kv_send.at[k, i, slot], kv_recv.at[k, i, slot],
            device,
        ).start()

    def share(k, i, r):
        spread(k, i, r, 3 + r, dev(x, y, z, sib))

    def arrived(k, i, r, core, slot):
        spot = piece(k, i, r, core)
        pltpu.make_async_copy(spot, spot, kv_recv.at[k, i, slot]).wait()

    right, left = dev((x + 1) % NX, y, z, c), dev((x + NX - 1) % NX, y, z, c)

    def neighbours(i):
        own = kv.at[:, :, 2 * x + i, c]
        pltpu.make_async_copy(own, own, a_recv.at[i]).wait()
        for k in range(2):
            spread(k, i, 0, 0, right)
            spread(k, i, 0, 2, left)
            share(k, i, 0)

    def relay(i):
        arrived(0, i, 1, c, 0)
        spread(0, i, 1, 1, right)
        share(0, i, 1)
        arrived(1, i, 3, c, 2)
        spread(1, i, 3, 1, left)
        share(1, i, 3)
        arrived(0, i, 3, c, 2)
        share(0, i, 3)
        arrived(1, i, 1, c, 0)
        share(1, i, 1)

    def far(i):
        for k in range(2):
            arrived(k, i, 2, c, 1)
            share(k, i, 2)

    def other(i, r):
        for k in range(2):
            arrived(k, i, r, sib, 3 + r)

    w_own.wait()
    w_sib.wait_recv()
    twin = dev(x, yhi * 2 + 1 - ylo, z, c)

    def w_copy(block, half, slot, device):
        spot = w_ref.at[block, half]
        remote(spot, spot, w_send.at[slot], w_recv.at[slot], device).start()

    def w_wait(block, half, slot):
        spot = w_ref.at[block, half]
        pltpu.make_async_copy(spot, spot, w_recv.at[slot]).wait()

    def above(s):
        return (z + s) % NZ

    def below(s):
        return (z - s + NZ) % NZ

    def forward(s):
        if s:
            w_wait(below(s), ylo, s)
            w_copy(below(s), ylo, 7 + s, twin)
            if s < 4:
                w_wait(above(s), ylo, 4 + s)
                w_copy(above(s), ylo, 11 + s, twin)
        if s < 4:
            w_copy(below(s), ylo, 1 + s, dev(x, y, above(1), c))
        if s < 3:
            w_copy(above(s), ylo, 5 + s, dev(x, y, below(1), c))

    def w_finish():
        for s in range(1, 5):
            w_wait(below(s), 1 - ylo, 7 + s)
            if s < 4:
                w_wait(above(s), 1 - ylo, 11 + s)

    neighbours(0)
    forward(0)
    relay(0)
    pltpu.make_async_copy(q_ref, q_ref, a_recv.at[2]).wait()

    m_ref[...] = jnp.full_like(m_ref, NEG)
    acc_ref[...] = jnp.zeros_like(acc_ref)

    def block(xs, i, js):
        g = 2 * xs + i
        keys = jnp.concatenate([kv[0, half, g].reshape(512, 128) for half in range(2)], axis=0)
        values = jnp.concatenate([kv[1, half, g].reshape(512, 128) for half in range(2)], axis=0)
        values = jnp.concatenate([values, jnp.ones_like(values)], axis=1)
        for j in js:
            query_clip = clip_ref[(j // 2) * 8 + 2 * x + j % 2]
            kept = [query_clip == clip_ref[half * 8 + g] for half in range(2)]
            s = lax.dot_general(
                q_ref[j // 2, j % 2], keys, (((1,), (1,)), ((), ())),
                preferred_element_type=F32,
            )
            s = [s[:, :512], s[:, 512:]]
            tops = [
                jnp.where(kept[half], jnp.max(s[half], axis=1, keepdims=True), NEG)
                for half in range(2)
            ]
            old = m_ref[j]
            new = jnp.maximum(old, jnp.maximum(tops[0], tops[1]) * coef)
            alpha = jnp.exp2(old - new)
            m_ref[j] = new
            p = [
                jnp.exp2(s[half] * coef - jnp.where(kept[half], new, -NEG)[:, :1]).astype(BF)
                for half in range(2)
            ]
            acc_ref[j] = acc_ref[j] * jnp.concatenate([alpha, alpha], axis=1) + jnp.dot(
                jnp.concatenate(p, axis=1), values, preferred_element_type=F32
            )

    order = ((0, 0), (1, 0), (3, 0), (0, 1), (2, 0), (1, 1), (3, 1), (2, 1))

    def pick(step, table):
        value = table[0]
        for n in range(1, len(table)):
            value = jnp.where(step == n, table[n], value)
        return value

    def attend(step, carry):
        @pl.when(step == 0)
        def _():
            other(0, 0)

        @pl.when(step == 1)
        def _():
            other(0, 1)

        @pl.when(step == 2)
        def _():
            other(0, 3)
            neighbours(1)

        @pl.when(step == 3)
        def _():
            far(0)
            other(1, 0)
            forward(1)

        @pl.when(step == 4)
        def _():
            other(0, 2)

        @pl.when(step == 5)
        def _():
            relay(1)
            other(1, 1)
            forward(2)

        @pl.when(step == 6)
        def _():
            other(1, 3)

        r = pick(step, [pair[0] for pair in order])
        block((x - r + NX) % NX, pick(step, [pair[1] for pair in order]), range(4))
        return carry

    lax.fori_loop(0, 7, attend, 0)
    far(1)
    other(1, 2)

    me = x * 2 + c
    mine = ylo ^ yhi
    head = pl.multiple_of((z * 2 + ylo) * 128, 128)

    def o_move(half):
        def go(n, carry):
            pair = (mine + n % 2) % 2
            zz = (z + hop(n // 2)) % NZ
            remote(
                o_ref.at[half, pair, zz], oa.at[me, pair ^ half, :, :, pl.ds(head, 128)],
                o_send.at[half], o_recv.at[half], dev(x, yhi * 2 + (pair ^ yhi), zz, c),
            ).start()
            return carry

        for i in range(2):
            acc = acc_ref[2 * half + i]
            o = (acc[:, :128] / acc[:, 128:]).astype(BF)
            for yh in range(2):
                o_ref[half, half ^ yh, :, i] = o[yh * 128:(yh + 1) * 128].reshape(NZ, 16, 128)
        pltpu.make_async_copy(
            o_ref.at[half, mine, z], oa.at[me, mine ^ half, :, :, pl.ds(head, 128)],
            o_recv.at[half],
        ).start()
        lax.fori_loop(1, 2 * NZ, go, 0)

    for half in range(2):
        block((x - 2 + NX) % NX, 1, (2 * half, 2 * half + 1))
        o_move(half)
    forward(3)

    def oa_spot(half, r, core, i=None):
        spot = oa.at[((x - r + NX) % NX) * 2 + core, mine ^ half]
        return spot if i is None else spot.at[i]

    def oa_copy(half, r, i, slot, device):
        spot = oa_spot(half, r, c, i)
        remote(spot, spot, oa_send.at[half, slot], oa_recv.at[half, slot], device).start()

    def oa_arrived(half, r, core, i, slot):
        spot = oa_spot(half, r, core, i)
        pltpu.make_async_copy(spot, spot, oa_recv.at[half, slot]).wait()

    def oa_share(half, r):
        oa_copy(half, r, None, 6 + r, dev(x, y, z, sib))

    for half in range(2):
        own = oa_spot(half, 0, c)
        pltpu.make_async_copy(own, own, o_recv.at[half]).wait()
        for i in range(2):
            oa_copy(half, 0, i, 3 * i, right)
            oa_copy(half, 0, i, 3 * i + 2, left)
        oa_share(half, 0)
    for half in range(2):
        oa_arrived(half, 1, c, 0, 0)
        oa_copy(half, 1, 0, 1, right)
        oa_arrived(half, 3, c, 1, 5)
        oa_copy(half, 3, 1, 4, left)
        oa_arrived(half, 1, c, 1, 3)
        oa_share(half, 1)
        oa_arrived(half, 3, c, 0, 2)
        oa_share(half, 3)
    forward(4)
    for half in range(2):
        oa_arrived(half, 2, c, 0, 1)
        oa_arrived(half, 2, c, 1, 4)
        oa_share(half, 2)
    w_finish()

    for half in range(2):
        for r in range(NX):
            oa_arrived(half, r, sib, None, 6 + r)
        h = mine ^ half
        part = jnp.dot(
            oa[:, h].reshape(256, 2048), w_ref[...].reshape(2048, cols),
            preferred_element_type=F32,
        )
        ps[pl.ds(8 * half, 8)] = part.astype(BF).reshape(8, 32, cols)
        land = pr.at[yhi, :, wcols(c)]

        def deliver(n, carry, half=half, h=h, land=land):
            xx = (x + n // 2) % NX
            core = (c + n) % 2
            spot = ps.at[8 * half + 2 * xx + core]
            here = jnp.logical_and(n == 0, h == yhi)

            @pl.when(here)
            def _():
                pltpu.make_async_copy(spot, land, p_recv).start()

            @pl.when(jnp.logical_not(here))
            def _():
                remote(
                    spot, land, p_send, p_recv, dev(xx, h * 2 + (mine ^ h), z, core)
                ).start()

            return carry

        lax.fori_loop(0, 8, deliver, 0)
    pltpu.make_async_copy(pr, pr, p_recv).wait()

    def left_here(spot, sem):
        pltpu.make_async_copy(spot, spot, sem).wait()

    for k in range(3):
        left_here(src.at[0, :, :, pl.ds(0, (NY * NZ - 1) * 128)], a_send.at[k])
    left_here(w_ref.at[z, c], w_send.at[0])
    for slot in range(1, 15):
        left_here(w_ref.at[z, ylo], w_send.at[slot])
    for k in range(2):
        for i in range(2):
            for slot in range(7):
                left_here(piece(k, i, 0, c), kv_send.at[k, i, slot])
    for half in range(2):
        left_here(oa.at[0, 0, :, :, pl.ds(0, (2 * NZ - 1) * 128)], o_send.at[half])
        for slot in range(10):
            left_here(oa_spot(half, 0, c, 0 if slot < 6 else None), oa_send.at[half, slot])
    sent = ps.at[pl.ds(0, 15)]
    pltpu.make_async_copy(sent, sent, p_send).wait()


def on_device(qkv, frame_clip, w_out):
    parts, tokens, width = qkv.shape
    rows, columns = w_out.shape
    cols = columns // 8
    dma = pltpu.SemaphoreType.DMA
    halves = pl.pallas_call(
        kernel,
        out_shape=jax.ShapeDtypeStruct((2, tokens, columns), BF),
        in_specs=[
            pl.BlockSpec(memory_space=pltpu.SMEM),
            pl.BlockSpec(memory_space=pl.ANY),
            pl.BlockSpec(memory_space=pl.ANY),
        ],
        out_specs=pl.BlockSpec(memory_space=pl.ANY),
        scratch_shapes=[
            pltpu.VMEM((3, 2, 16, width), BF),
            pltpu.VMEM((2, 2, 256, 128), BF),
            pltpu.VMEM((2, 2, 8, 2, 256, 128), BF),
            pltpu.VMEM((NZ, 2, rows, cols), BF),
            pltpu.VMEM((4, 256, 128), F32),
            pltpu.VMEM((4, 256, 256), F32),
            pltpu.VMEM((2, 2, NZ, 2, 16, 128), BF),
            pltpu.VMEM((8, 2, 2, 16, 2048), BF),
            pltpu.VMEM((16, 32, cols), BF),
            dma((2,)), dma((3,)), dma((3,)), dma((2, 2, 7)), dma((2, 2, 7)), dma((15,)), dma((15,)),
            dma((2,)), dma((2,)), dma((2, 10)), dma((2, 10)), dma, dma,
        ],
        compiler_params=pltpu.CompilerParams(
            collective_id=0, has_side_effects=True, vmem_limit_bytes=66_400_000
        ),
        name="attend_and_project",
    )(frame_clip, qkv.reshape(parts, 2, tokens // 2, width), w_out)
    return (halves[0].astype(F32) + halves[1].astype(F32)).astype(BF)


def solution(mesh):
    in_specs = (P(None, ("blk", "tile"), None), P(), P("tile", None))
    out_specs = P(("blk", "tile"), None)
    return jax.shard_map(
        on_device, mesh=mesh, in_specs=in_specs, out_specs=out_specs, check_vma=False
    )
```

time: 88.4 us -> 83.5 us (0.945)
  Pallas kernels: 86.5 us -> 80.7 us
  other arithmetic: 0 us -> 1.87 us
  local copies, waits for them, and re-layouts: 1.72 us -> 0 us
    pallas_call x1, Pallas kernels: 86.5 us -> 80.7 us  [on_device(): pl.pallas_call(kernel, out_shape=jax.ShapeDtypeStruct((2, tokens, columns...]
    convert_element_type x0 -> x1, other arithmetic: none -> 1.87 us  [on_device(): return (halves[0].astype(F32) + halves[1].astype(F32)).astype(BF)]
    unnamed x1 -> x0, local copies, waits for them, and re-layouts: 1.72 us -> none
where the time goes in v3:
time: 83.5 us; the launch traced here: 82.6 us
  Pallas kernels  80.7 us (97%)
  other arithmetic  1.87 us (2%)
    pallas_call x1, Pallas kernels, on_device(): pl.pallas_call(kernel, out_shape=jax.ShapeDtypeStruct((2, tokens, columns...  80.7 us
    convert_element_type x1, other arithmetic, on_device(): return (halves[0].astype(F32) + halves[1].astype(F32)).astype(BF)  1.87 us

profile of v3, /device:TPU:1, one launch (start us, length us, event | category | flops | bytes accessed | tf_op | source)
XLA Modules:
  0.0 82.6 jit_solution(9454787408826402781)
XLA Ops:
  0.0 80.7 %attend_and_project.1 = bf16[2,32,5120]{2,1,0:T(8,128)(2,1)} custom-call(s32[16]{0:T(128)} %clip_ref.1, bf16[3,2,16,4096]{3,2,1,0:T(8,128)(2,1)} %bitcast.3, bf16[128,5120]{1,0:T(8,128)(2,1)} %w_in.1), custom_call_target="tpu_custom_call" | custom-call | tf_op jit(solution)/shard_map/attend_and_project/pallas_call | solution.py:417
  80.8 1.9 %fusion = bf16[32,5120]{1,0:T(8,128)(2,1)} fusion(bf16[2,32,5120]{2,1,0:T(8,128)(2,1)} %attend_and_project.1), kind=kLoop, calls=%fused_computation.1 | loop fusion | flops 655360 | bytes 983040 | tf_op jit(solution)/shard_map/convert_element_type | solution.py:444

commit v4 on v3

--- a/solution.py
+++ b/solution.py
@@ -95,7 +95,7 @@
 
     def scatter(k):
         def send(n, carry):
-            yy, zz = plane(n)
+            yy, zz = plane(NY * NZ - n)
             remote(
                 cut(k, column(yy, zz)), landing(k), a_send.at[k], a_recv.at[k],
                 dev(x, yy, zz, c),
@@ -295,6 +295,7 @@
 
     def o_move(half):
         def go(n, carry):
+            n = 2 * NZ - n
             pair = (mine + n % 2) % 2
             zz = (z + hop(n // 2)) % NZ
             remote(

time: 83.5 us -> 81 us (0.970)
  Pallas kernels: 80.7 us -> 78.6 us
    pallas_call x1, Pallas kernels: 80.7 us -> 78.6 us  [on_device(): pl.pallas_call(kernel, out_shape=jax.ShapeDtypeStruct((2, tokens, columns...]
where the time goes in v4:
time: 81 us; the launch traced here: 80.5 us
  Pallas kernels  78.6 us (97%)
  other arithmetic  1.87 us (2%)
    pallas_call x1, Pallas kernels, on_device(): pl.pallas_call(kernel, out_shape=jax.ShapeDtypeStruct((2, tokens, columns...  78.6 us
    convert_element_type x1, other arithmetic, on_device(): return (halves[0].astype(F32) + halves[1].astype(F32)).astype(BF)  1.87 us

profile of v4, /device:TPU:1, one launch (start us, length us, event | category | flops | bytes accessed | tf_op | source)
XLA Modules:
  0.0 80.5 jit_solution(8303170848416628227)
XLA Ops:
  0.0 78.6 %attend_and_project.1 = bf16[2,32,5120]{2,1,0:T(8,128)(2,1)} custom-call(s32[16]{0:T(128)} %clip_ref.1, bf16[3,2,16,4096]{3,2,1,0:T(8,128)(2,1)} %bitcast.3, bf16[128,5120]{1,0:T(8,128)(2,1)} %w_in.1), custom_call_target="tpu_custom_call" | custom-call | tf_op jit(solution)/shard_map/attend_and_project/pallas_call | solution.py:418
  78.6 1.9 %fusion = bf16[32,5120]{1,0:T(8,128)(2,1)} fusion(bf16[2,32,5120]{2,1,0:T(8,128)(2,1)} %attend_and_project.1), kind=kLoop, calls=%fused_computation.1 | loop fusion | flops 655360 | bytes 983040 | tf_op jit(solution)/shard_map/convert_element_type | solution.py:445

commit v5 on v4

--- a/solution.py
+++ b/solution.py
@@ -370,6 +370,7 @@
         land = pr.at[yhi, :, wcols(c)]
 
         def deliver(n, carry, half=half, h=h, land=land):
+            n = 7 - n
             xx = (x + n // 2) % NX
             core = (c + n) % 2
             spot = ps.at[8 * half + 2 * xx + core]

time: 81 us -> 80.7 us (level)
  no operation moved by 1% of the time
where the time goes in v5:
time: 80.7 us; the launch traced here: 79.7 us
  Pallas kernels  77.8 us (96%)
  other arithmetic  1.87 us (2%)
    pallas_call x1, Pallas kernels, on_device(): pl.pallas_call(kernel, out_shape=jax.ShapeDtypeStruct((2, tokens, columns...  77.8 us
    convert_element_type x1, other arithmetic, on_device(): return (halves[0].astype(F32) + halves[1].astype(F32)).astype(BF)  1.87 us

profile of v5, /device:TPU:1, one launch (start us, length us, event | category | flops | bytes accessed | tf_op | source)
XLA Modules:
  0.0 79.7 jit_solution(17418966159333591169)
XLA Ops:
  0.0 77.8 %attend_and_project.1 = bf16[2,32,5120]{2,1,0:T(8,128)(2,1)} custom-call(s32[16]{0:T(128)} %clip_ref.1, bf16[3,2,16,4096]{3,2,1,0:T(8,128)(2,1)} %bitcast.3, bf16[128,5120]{1,0:T(8,128)(2,1)} %w_in.1), custom_call_target="tpu_custom_call" | custom-call | tf_op jit(solution)/shard_map/attend_and_project/pallas_call | solution.py:419
  77.8 1.9 %fusion = bf16[32,5120]{1,0:T(8,128)(2,1)} fusion(bf16[2,32,5120]{2,1,0:T(8,128)(2,1)} %attend_and_project.1), kind=kLoop, calls=%fused_computation.1 | loop fusion | flops 655360 | bytes 983040 | tf_op jit(solution)/shard_map/convert_element_type | solution.py:446
